TPU v7x, 32 devices: a whole 2x2x4 slice. The times are simulated.
32 devices in a mesh: groups: 2 (over y), ctx: 8 (over z, x), chan: 2 (over core).
Axes of the slice: x: 2, y: 2, z: 4, core: 2. Of those that a mesh axis runs over, the one named last changes fastest.
Arguments:
- inputs: bfloat16 [2048, 2048], P(('groups', 'ctx'), 'chan'), parts along dimension 0, may hold values from -0.1875 to 0.1875
- out_grad: bfloat16 [2048, 2048], P(('groups', 'ctx'), 'chan'), parts along dimension 0, may hold values from -6 to 6
- filters: bfloat16 [512, 2048], P(None, 'chan'), may hold values from -0.25 to 0.25
Outputs:
- in_grad: bfloat16 [2048, 2048], P(('groups', 'ctx'), 'chan'), parts along dimension 0
- filter_grad: float32 [1024, 2048], P(('groups', 'ctx'), 'chan'), parts along dimension 0
There are 2 independent parts, one for each index of `groups`. A program takes and returns all parts, laid end to end along the dimension named above; an argument that names none is the same for every part. Nothing has to cross between parts.
All inputs are finite; a program needn't handle non-finite values.
Results may differ from a plain program's by a relative error of at most 0.0085.
Values may be sent and summed in bfloat16 or wider, within the bound.
A program may use at most 64 MiB of HBM per device.

v0:
```python
import functools
import math

import jax
import jax.numpy as jnp
import numpy as np
from jax import lax
from jax.experimental import pallas as pl
from jax.experimental.pallas import tpu as pltpu
from jax.sharding import PartitionSpec as P

LANES = 128
CHUNK = 16


def passed_along(value, axis, steps):
    count = lax.axis_size(axis)
    initial, last = (max(0, -steps), min(count, count - steps))
    return lax.ppermute(value, axis, [(source, source + steps) for source in range(initial, last)])


def phase_table(row_ids, col_ids, period):
    return 2.0 * math.pi / period * (row_ids * col_ids % period).astype(jnp.float32)


def split_table(table):
    high_part = table.astype(jnp.bfloat16)
    low_part = (table - high_part.astype(jnp.float32)).astype(jnp.bfloat16)
    return (high_part, low_part)


def forward_apply(parts, data):
    first = jnp.dot(parts[0], data, preferred_element_type=jnp.float32)
    return first + jnp.dot(parts[1], data, preferred_element_type=jnp.float32)


def spectral(table, data):
    return jnp.dot(table, data, precision=lax.Precision.HIGH, preferred_element_type=jnp.float32)


def general_plan(inputs, out_grad, filters):
    tok_len = out_grad.shape[0]
    channels = out_grad.shape[1]
    lag_count = filters.shape[0]
    far_reach = lag_count // tok_len
    period = 2 * tok_len
    freq_count = tok_len + 1
    freq_col = jnp.arange(freq_count, dtype=jnp.int32)[:, None]
    time_row = jnp.arange(tok_len, dtype=jnp.int32)[None, :]
    angle_fwd = phase_table(freq_col, time_row, period)
    forward = split_table(jnp.concatenate([jnp.cos(angle_fwd), -jnp.sin(angle_fwd)], axis=0))
    freq_row = jnp.arange(freq_count, dtype=jnp.int32)[None, :]
    weighting = (
        jnp.where((freq_row == 0) | (freq_row == tok_len), 1.0, 2.0).astype(jnp.float32) / period
    )
    back_rows = (tok_len - jnp.arange(tok_len, dtype=jnp.int32))[:, None]
    angle_back = phase_table(back_rows, freq_row, period)
    inverse_in = jnp.concatenate(
        [weighting * jnp.cos(angle_back), -weighting * jnp.sin(angle_back)], axis=1
    )
    lag_rows = ((jnp.arange(period, dtype=jnp.int32) - tok_len) % period)[:, None]
    angle_lag = phase_table(lag_rows, freq_row, period)
    inverse_lag = jnp.concatenate(
        [weighting * jnp.cos(angle_lag), -weighting * jnp.sin(angle_lag)], axis=1
    )
    parity = jnp.where(jnp.arange(freq_count) % 2 == 0, 1.0, -1.0).astype(jnp.float32)
    parity_both = jnp.concatenate([parity, parity])[:, None]
    received = [out_grad]
    current = out_grad
    for offset in range(far_reach):
        current = passed_along(current, "ctx", -1)
        received.append(current)
    tap_blocks = filters.reshape(far_reach, tok_len, channels)
    tap_spec = jnp.einsum("ft,btc->bfc", forward[0], tap_blocks, preferred_element_type=jnp.float32)
    tap_spec = tap_spec + jnp.einsum(
        "ft,btc->bfc", forward[1], tap_blocks, preferred_element_type=jnp.float32
    )
    input_spec = forward_apply(forward, inputs)
    input_re = input_spec[:freq_count]
    input_im = input_spec[freq_count:]
    accum_re = jnp.zeros((freq_count, channels), jnp.float32)
    accum_im = jnp.zeros((freq_count, channels), jnp.float32)
    lag_parts = []
    for offset in range(far_reach + 1):
        grad_spec = forward_apply(forward, received[offset])
        grad_re = grad_spec[:freq_count]
        grad_im = grad_spec[freq_count:]
        if offset >= 1 and offset < far_reach:
            segment = tap_spec[offset - 1] + parity_both * tap_spec[offset]
        elif offset >= 1:
            segment = tap_spec[offset - 1]
        else:
            segment = parity_both * tap_spec[offset]
        seg_re = segment[:freq_count]
        seg_im = segment[freq_count:]
        accum_re = accum_re + grad_re * seg_re + grad_im * seg_im
        accum_im = accum_im + grad_re * seg_im - grad_im * seg_re
        cross = jnp.concatenate(
            [grad_re * input_re + grad_im * input_im, grad_im * input_re - grad_re * input_im],
            axis=0,
        )
        lag_parts.append(spectral(inverse_lag, cross))
    in_grad = spectral(inverse_in, jnp.concatenate([accum_re, accum_im], axis=0)).astype(
        jnp.bfloat16
    )
    segments = [
        lag_parts[index + 1][:tok_len] + lag_parts[index][tok_len:] for index in range(far_reach)
    ]
    partial_value = jnp.concatenate(segments, axis=0)
    filter_grad = lax.psum_scatter(partial_value, "ctx", scatter_dimension=0, tiled=True)
    return (in_grad, filter_grad)


def table_parts(table):
    high_part = table.astype(jnp.bfloat16)
    low_part = (table - high_part.astype(np.float64)).astype(jnp.bfloat16)
    return np.stack([high_part, low_part])


def transform_tables(block):
    order = np.concatenate([np.arange(0, block, 2), np.arange(1, block, 2)])
    steps = (2 * order + 1)[:, None] * np.arange(block)[None, :] % (4 * block)
    angle = np.pi / (2 * block) * steps
    forward = np.concatenate([np.cos(angle), np.sin(angle)], axis=0)
    return table_parts(forward), table_parts(forward.T / block)


def peer_order(count):
    return sorted(range(1, count), key=lambda step: (-abs(2 * step - count), step))


def exchange_kernel(
    count, block,
    in_ref, grad_ref, taps_ref, fwd_hbm, inv_hbm,
    out_ref, lag_ref,
    u_buf, g_buf, tap_buf, fwd, inv, g_spec, u_spec, tap_spec, seg_spec, r_high, r_low, q_high, q_low,
    out_buf, lag_buf, send_sem, recv_sem, local_sem,
):
    me = lax.axis_index("ctx")
    tok_len = in_ref.shape[0]
    width = g_buf.shape[2]
    lag_count = taps_ref.shape[0]
    own_lags = lag_count // count
    per_block = block // tok_len
    blocks = g_buf.shape[0]
    segs = lag_count // block
    order = peer_order(count)

    def cols(index):
        return pl.ds(pl.multiple_of(index * width, LANES), width)

    def place(buf, index):
        rows = pl.ds(pl.multiple_of(lax.rem(index, per_block) * tok_len, tok_len), tok_len)
        return buf.at[lax.div(index, per_block), rows, :]

    my_cols = cols(me)
    local = [
        pltpu.make_async_copy(fwd_hbm, fwd, local_sem.at[0]),
        pltpu.make_async_copy(taps_ref.at[:, my_cols], tap_buf, local_sem.at[1]),
        pltpu.make_async_copy(grad_ref.at[:, my_cols], place(g_buf, me), local_sem.at[2]),
        pltpu.make_async_copy(in_ref.at[:, my_cols], place(u_buf, me), local_sem.at[3]),
        pltpu.make_async_copy(inv_hbm, inv, local_sem.at[4]),
    ]
    barrier = pltpu.get_barrier_semaphore()
    for step in order:
        pl.semaphore_signal(
            barrier, inc=1, device_id={"ctx": lax.rem(me + step, count)},
            device_id_type=pl.DeviceIdType.MESH,
        )
    for copy in local:
        copy.start()
    pl.semaphore_wait(barrier, count - 1)

    def send_all(kind, source, target):
        copies = []
        for step in order if kind % 2 == 0 else order[::-1]:
            peer = lax.rem(me + step, count)
            copies.append(
                pltpu.make_async_remote_copy(
                    src_ref=source(peer),
                    dst_ref=target,
                    send_sem=send_sem.at[kind, step],
                    recv_sem=recv_sem.at[kind, step],
                    device_id={"ctx": peer},
                    device_id_type=pl.DeviceIdType.MESH,
                )
            )
            copies[-1].start()
        return copies

    g_copies = send_all(0, lambda peer: grad_ref.at[:, cols(peer)], place(g_buf, me))
    u_copies = send_all(1, lambda peer: in_ref.at[:, cols(peer)], place(u_buf, me))

    def forward(data):
        first = jnp.dot(fwd[0], data, preferred_element_type=jnp.float32)
        return first + jnp.dot(fwd[1], data, preferred_element_type=jnp.float32)

    def inverse(high, low):
        first = jnp.dot(inv[0], high, preferred_element_type=jnp.float32)
        second = jnp.dot(inv[1], high, preferred_element_type=jnp.float32)
        return first + (second + jnp.dot(inv[0], low, preferred_element_type=jnp.float32))

    def lanes(index):
        return slice(index * width, (index + 1) * width)

    def over_chunks(body):
        half = block // 2 // CHUNK
        for sign, start in ((1.0, 0), (-1.0, half)):
            def step(index, carry, sign=sign):
                row = pl.multiple_of(index * CHUNK, CHUNK)
                body(pl.ds(row, CHUNK), pl.ds(row + block, CHUNK), sign)
                return carry
            lax.fori_loop(start, start + half, step, 0)

    def store_split(high, low, rows, where, value):
        top = value.astype(jnp.bfloat16)
        high[rows, where] = top
        low[rows, where] = (value - top.astype(jnp.float32)).astype(jnp.bfloat16)

    local[0].wait()
    local[1].wait()
    tap_spec[...] = forward(
        jnp.concatenate([tap_buf[s * block:(s + 1) * block, :] for s in range(segs)], axis=1)
    )

    def segment_chunk(re, im, sign):
        for d in range(segs + 1):
            real = imag = 0.0
            if d < segs:
                real, imag = tap_spec[re, lanes(d)], tap_spec[im, lanes(d)]
            if d > 0:
                real = real + sign * tap_spec[im, lanes(d - 1)]
                imag = imag - sign * tap_spec[re, lanes(d - 1)]
            seg_spec[re, lanes(d)] = real
            seg_spec[im, lanes(d)] = imag

    over_chunks(segment_chunk)

    local[2].wait()
    for copy in g_copies:
        copy.wait_recv()
    g_spec[...] = forward(jnp.concatenate([g_buf[b] for b in range(blocks)], axis=1))

    def in_chunk(re, im, sign):
        grads = [(g_spec[re, lanes(b)], g_spec[im, lanes(b)]) for b in range(blocks)]
        taps = [(seg_spec[re, lanes(d)], seg_spec[im, lanes(d)]) for d in range(segs + 1)]
        for b in range(blocks):
            real = imag = 0.0
            for d in range(min(segs + 1, blocks - b)):
                gr, gi = grads[b + d]
                hr, hi = taps[d]
                real = real + (gr * hr + gi * hi)
                imag = imag + (gi * hr - gr * hi)
            store_split(r_high, r_low, re, lanes(b), real)
            store_split(r_high, r_low, im, lanes(b), imag)

    over_chunks(in_chunk)
    local[4].wait()
    result = inverse(r_high[...], r_low[...]).astype(jnp.bfloat16)
    for index in range(count):
        rows = index % per_block * tok_len
        out_buf[index] = result[rows:rows + tok_len, lanes(index // per_block)]
    out_copies = send_all(2, lambda peer: out_buf.at[peer], out_ref.at[:, my_cols])
    own_out = pltpu.make_async_copy(out_buf.at[me], out_ref.at[:, my_cols], local_sem.at[5])
    own_out.start()

    local[3].wait()
    for copy in u_copies:
        copy.wait_recv()
    u_spec[...] = forward(jnp.concatenate([u_buf[b] for b in range(blocks)], axis=1))

    def lag_chunk(re, im, sign):
        grads = [(g_spec[re, lanes(b)], g_spec[im, lanes(b)]) for b in range(blocks)]
        values = [(u_spec[re, lanes(b)], u_spec[im, lanes(b)]) for b in range(blocks)]
        cross = []
        for d in range(segs + 1):
            real = imag = jnp.zeros((CHUNK, width), jnp.float32)
            for b in range(d, blocks):
                gr, gi = grads[b]
                ur, ui = values[b - d]
                real = real + (gr * ur + gi * ui)
                imag = imag + (gi * ur - gr * ui)
            cross.append((real, imag))
        for s in range(segs):
            store_split(q_high, q_low, re, lanes(s), cross[s][0] - sign * cross[s + 1][1])
            store_split(q_high, q_low, im, lanes(s), cross[s][1] + sign * cross[s + 1][0])

    over_chunks(lag_chunk)
    lag_result = inverse(q_high[...], q_low[...]).astype(jnp.bfloat16)
    for index in range(count):
        rows = index * own_lags % block
        lag_buf[index] = lag_result[rows:rows + own_lags, lanes(index * own_lags // block)]
    lag_copies = send_all(3, lambda peer: lag_buf.at[peer], lag_ref.at[:, my_cols])
    own_lag = pltpu.make_async_copy(lag_buf.at[me], lag_ref.at[:, my_cols], local_sem.at[6])
    own_lag.start()

    for copy in g_copies + u_copies:
        copy.wait_send()
    own_out.wait()
    own_lag.wait()
    for copy in out_copies + lag_copies:
        copy.wait()


def finish_kernel(in_ref, lag_ref, in_out, lag_out, lag_wide, sem):
    move = pltpu.make_async_copy(in_ref, in_out, sem.at[0])
    move.start()
    lag_wide[...] = lag_ref[...].astype(lag_wide.dtype)
    store = pltpu.make_async_copy(lag_wide, lag_out, sem.at[1])
    store.start()
    move.wait()
    store.wait()


def block_length(tok_len, count, lag_count):
    block = tok_len
    if count % 2 == 0 and lag_count % (2 * tok_len) == 0:
        block = 2 * tok_len
    return block


def whole_lanes(tok_len, channels, lag_count, count):
    block = block_length(tok_len, count, lag_count)
    return (
        count > 1
        and channels % (count * LANES) == 0
        and tok_len % CHUNK == 0
        and block % (2 * CHUNK) == 0
        and lag_count % block == 0
        and lag_count % (count * CHUNK) == 0
        and block % (lag_count // count) == 0
        and count * tok_len <= 4 * lag_count
    )


def per_device(inputs, out_grad, filters):
    tok_len, channels = out_grad.shape
    lag_count = filters.shape[0]
    count = lax.axis_size("ctx")
    if not whole_lanes(tok_len, channels, lag_count, count):
        return general_plan(inputs, out_grad, filters)
    block = block_length(tok_len, count, lag_count)
    width = channels // count
    blocks = count * tok_len // block
    segs = lag_count // block
    own_lags = lag_count // count
    fwd, inv = transform_tables(block)
    bf16, f32 = jnp.bfloat16, jnp.float32
    anywhere = pl.BlockSpec(memory_space=pl.ANY)
    in_vmem = pl.BlockSpec(memory_space=pltpu.VMEM)
    in_grad, lag_grad = pl.pallas_call(
        functools.partial(exchange_kernel, count, block),
        out_shape=(
            pltpu.VMEM((tok_len, channels), bf16),
            pltpu.VMEM((own_lags, channels), bf16),
        ),
        in_specs=[anywhere] * 5,
        out_specs=(in_vmem, in_vmem),
        scratch_shapes=[
            pltpu.VMEM((blocks, block, width), bf16),
            pltpu.VMEM((blocks, block, width), bf16),
            pltpu.VMEM((lag_count, width), bf16),
            pltpu.VMEM(fwd.shape, bf16),
            pltpu.VMEM(inv.shape, bf16),
            pltpu.VMEM((2 * block, blocks * width), f32),
            pltpu.VMEM((2 * block, blocks * width), f32),
            pltpu.VMEM((2 * block, segs * width), f32),
            pltpu.VMEM((2 * block, (segs + 1) * width), f32),
            pltpu.VMEM((2 * block, blocks * width), bf16),
            pltpu.VMEM((2 * block, blocks * width), bf16),
            pltpu.VMEM((2 * block, segs * width), bf16),
            pltpu.VMEM((2 * block, segs * width), bf16),
            pltpu.VMEM((count, tok_len, width), bf16),
            pltpu.VMEM((count, own_lags, width), bf16),
            pltpu.SemaphoreType.DMA((4, count)),
            pltpu.SemaphoreType.DMA((4, count)),
            pltpu.SemaphoreType.DMA((7,)),
        ],
        compiler_params=pltpu.CompilerParams(collective_id=0, has_side_effects=True),
    )(inputs, out_grad, filters, jnp.asarray(fwd), jnp.asarray(inv))
    return pl.pallas_call(
        finish_kernel,
        out_shape=(
            jax.ShapeDtypeStruct(in_grad.shape, bf16),
            jax.ShapeDtypeStruct(lag_grad.shape, f32),
        ),
        in_specs=[in_vmem, in_vmem],
        out_specs=(anywhere, anywhere),
        scratch_shapes=[
            pltpu.VMEM(lag_grad.shape, f32),
            pltpu.SemaphoreType.DMA((2,)),
        ],
    )(
        pltpu.with_memory_space_constraint(in_grad, pltpu.VMEM),
        pltpu.with_memory_space_constraint(lag_grad, pltpu.VMEM),
    )


def solution(mesh):
    return jax.shard_map(
        per_device,
        mesh=mesh,
        in_specs=(P(("groups", "ctx"), "chan"), P(("groups", "ctx"), "chan"), P(None, "chan")),
        out_specs=(P(("groups", "ctx"), "chan"), P(("groups", "ctx"), "chan")),
        check_vma=False,
    )
```

profile of v0, /device:TPU:0, one launch (start us, length us, event | category | flops | bytes accessed | tf_op | source)
XLA Modules:
  0.0 28.8 jit_solution(10647690896096254705)
XLA Ops:
  0.6 27.4 %shard_map.68 = (bf16[128,1024]{1,0:T(8,128)(2,1)S(1)}, bf16[64,1024]{1,0:T(8,128)(2,1)S(1)}) custom-call(bf16[128,1024]{1,0:T(8,128)(2,1)} %in_ref.1, bf16[128,1024]{1,0:T(8,128)(2,1)} %grad_ref.1, bf16[512,1024]{1,0:T(8,128)(2,1)} %taps_ref.1, bf16[2,512,256]{2,1,0:T(8,128)(2,1)} %constant.4.clone.fwd_hbm, bf16[2,256,512]{2,1,0:T(8,128)(2,1)} %constant.5.clone.inv_hbm), custom_call_target="tpu_custom_call" | custom-call | tf_op jit(solution)/shard_map/pallas_call | solution.py:351
  28.0 0.8 %shard_map.69 = (bf16[128,1024]{1,0:T(8,128)(2,1)}, f32[64,1024]{1,0:T(8,128)}) custom-call(bf16[128,1024]{1,0:T(8,128)(2,1)S(1)} %get-tuple-element.4.in_ref, bf16[64,1024]{1,0:T(8,128)(2,1)S(1)} %get-tuple-element.5.lag_ref), custom_call_target="tpu_custom_call" | custom-call | tf_op jit(solution)/shard_map/pallas_call | solution.py:381
where the time goes:
time: 29 us; the launch traced here: 28.8 us
  Pallas kernels  28.2 us (97%)
  between operations  0.64 us (2%)
    pallas_call x1, Pallas kernels, per_device(): pl.pallas_call(functools.partial(exchange_kernel, count, block), out_shap...  27.4 us
    pallas_call x1, Pallas kernels, per_device(): pl.pallas_call(finish_kernel, out_shape=(jax.ShapeDtypeStruct(in_grad.sha...  0.81 us

commit v1 on v0

v1 whole, which is shorter than its diff:
```python
import functools
import math

import jax
import jax.numpy as jnp
import numpy as np
from jax import lax
from jax.experimental import pallas as pl
from jax.experimental.pallas import tpu as pltpu
from jax.sharding import PartitionSpec as P

LANES = 128
CHUNK = 16
CHUNKS = 2


def passed_along(value, axis, steps):
    count = lax.axis_size(axis)
    initial, last = (max(0, -steps), min(count, count - steps))
    return lax.ppermute(value, axis, [(source, source + steps) for source in range(initial, last)])


def phase_table(row_ids, col_ids, period):
    return 2.0 * math.pi / period * (row_ids * col_ids % period).astype(jnp.float32)


def split_table(table):
    high_part = table.astype(jnp.bfloat16)
    low_part = (table - high_part.astype(jnp.float32)).astype(jnp.bfloat16)
    return (high_part, low_part)


def forward_apply(parts, data):
    first = jnp.dot(parts[0], data, preferred_element_type=jnp.float32)
    return first + jnp.dot(parts[1], data, preferred_element_type=jnp.float32)


def spectral(table, data):
    return jnp.dot(table, data, precision=lax.Precision.HIGH, preferred_element_type=jnp.float32)


def general_plan(inputs, out_grad, filters):
    tok_len = out_grad.shape[0]
    channels = out_grad.shape[1]
    lag_count = filters.shape[0]
    far_reach = lag_count // tok_len
    period = 2 * tok_len
    freq_count = tok_len + 1
    freq_col = jnp.arange(freq_count, dtype=jnp.int32)[:, None]
    time_row = jnp.arange(tok_len, dtype=jnp.int32)[None, :]
    angle_fwd = phase_table(freq_col, time_row, period)
    forward = split_table(jnp.concatenate([jnp.cos(angle_fwd), -jnp.sin(angle_fwd)], axis=0))
    freq_row = jnp.arange(freq_count, dtype=jnp.int32)[None, :]
    weighting = (
        jnp.where((freq_row == 0) | (freq_row == tok_len), 1.0, 2.0).astype(jnp.float32) / period
    )
    back_rows = (tok_len - jnp.arange(tok_len, dtype=jnp.int32))[:, None]
    angle_back = phase_table(back_rows, freq_row, period)
    inverse_in = jnp.concatenate(
        [weighting * jnp.cos(angle_back), -weighting * jnp.sin(angle_back)], axis=1
    )
    lag_rows = ((jnp.arange(period, dtype=jnp.int32) - tok_len) % period)[:, None]
    angle_lag = phase_table(lag_rows, freq_row, period)
    inverse_lag = jnp.concatenate(
        [weighting * jnp.cos(angle_lag), -weighting * jnp.sin(angle_lag)], axis=1
    )
    parity = jnp.where(jnp.arange(freq_count) % 2 == 0, 1.0, -1.0).astype(jnp.float32)
    parity_both = jnp.concatenate([parity, parity])[:, None]
    received = [out_grad]
    current = out_grad
    for offset in range(far_reach):
        current = passed_along(current, "ctx", -1)
        received.append(current)
    tap_blocks = filters.reshape(far_reach, tok_len, channels)
    tap_spec = jnp.einsum("ft,btc->bfc", forward[0], tap_blocks, preferred_element_type=jnp.float32)
    tap_spec = tap_spec + jnp.einsum(
        "ft,btc->bfc", forward[1], tap_blocks, preferred_element_type=jnp.float32
    )
    input_spec = forward_apply(forward, inputs)
    input_re = input_spec[:freq_count]
    input_im = input_spec[freq_count:]
    accum_re = jnp.zeros((freq_count, channels), jnp.float32)
    accum_im = jnp.zeros((freq_count, channels), jnp.float32)
    lag_parts = []
    for offset in range(far_reach + 1):
        grad_spec = forward_apply(forward, received[offset])
        grad_re = grad_spec[:freq_count]
        grad_im = grad_spec[freq_count:]
        if offset >= 1 and offset < far_reach:
            segment = tap_spec[offset - 1] + parity_both * tap_spec[offset]
        elif offset >= 1:
            segment = tap_spec[offset - 1]
        else:
            segment = parity_both * tap_spec[offset]
        seg_re = segment[:freq_count]
        seg_im = segment[freq_count:]
        accum_re = accum_re + grad_re * seg_re + grad_im * seg_im
        accum_im = accum_im + grad_re * seg_im - grad_im * seg_re
        cross = jnp.concatenate(
            [grad_re * input_re + grad_im * input_im, grad_im * input_re - grad_re * input_im],
            axis=0,
        )
        lag_parts.append(spectral(inverse_lag, cross))
    in_grad = spectral(inverse_in, jnp.concatenate([accum_re, accum_im], axis=0)).astype(
        jnp.bfloat16
    )
    segments = [
        lag_parts[index + 1][:tok_len] + lag_parts[index][tok_len:] for index in range(far_reach)
    ]
    partial_value = jnp.concatenate(segments, axis=0)
    filter_grad = lax.psum_scatter(partial_value, "ctx", scatter_dimension=0, tiled=True)
    return (in_grad, filter_grad)


def table_parts(table):
    high_part = table.astype(jnp.bfloat16)
    low_part = (table - high_part.astype(np.float64)).astype(jnp.bfloat16)
    return np.stack([high_part, low_part])


def transform_tables(block):
    order = np.concatenate([np.arange(0, block, 2), np.arange(1, block, 2)])
    steps = (2 * order + 1)[:, None] * np.arange(block)[None, :] % (4 * block)
    angle = np.pi / (2 * block) * steps
    forward = np.concatenate([np.cos(angle), np.sin(angle)], axis=0)
    return table_parts(forward), table_parts(forward.T / block)


def wait_for(like, sem):
    pltpu.make_async_copy(like, like, sem).wait()


def chain_kernel(
    pair, block, chunks,
    in_ref, grad_ref, taps_ref, fwd_hbm, inv_hbm,
    out_ref, lag_ref,
    g_buf, u_buf, tap_buf, fwd, inv, g_spec, u_spec, tap_spec, r_high, r_low, in_buf, part, own_low, next_low,
    gx_sem, ux_sem, direct_sem, passed_sem, far_sem, left_u_sem, low_sem, lag_sem, out_sem, send_sem, local_sem,
    ready, ready_far,
):
    me = lax.axis_index("ctx")
    level = lax.div(me, pair)
    side = lax.rem(me, pair)
    mate = me + 1 - 2 * side
    left, right = me - pair, me + pair
    tok_len, channels = in_ref.shape
    lag_count = taps_ref.shape[0]
    width = g_buf.shape[3]
    half = chunks * width
    segs = lag_count // block
    levels = 2 * segs
    own_lags = lag_count // (levels * pair)

    def cols(which, c):
        return pl.ds(pl.multiple_of(which * half + c * width, LANES), width)

    def rows(which, length):
        return pl.ds(pl.multiple_of(which * length, length), length)

    mine, other = rows(side, tok_len), rows(1 - side, tok_len)

    def remote(source, target, send, recv, device):
        pltpu.make_async_remote_copy(
            src_ref=source, dst_ref=target, send_sem=send, recv_sem=recv,
            device_id={"ctx": device}, device_id_type=pl.DeviceIdType.MESH,
        ).start()

    def signal(sem, device):
        pl.semaphore_signal(
            sem, inc=1, device_id={"ctx": device}, device_id_type=pl.DeviceIdType.MESH
        )

    def at_level(*which):
        hit = level == which[0]
        for value in which[1:]:
            hit = jnp.logical_or(hit, level == value)
        return pl.when(hit)

    barrier = pltpu.get_barrier_semaphore()
    signal(barrier, mate)

    @pl.when(level < levels - 1)
    def _():
        signal(barrier, right)

    pltpu.make_async_copy(taps_ref.at[:, rows_of_half(side, half)], tap_buf, local_sem.at[1]).start()
    pltpu.make_async_copy(fwd_hbm, fwd, local_sem.at[0]).start()
    for c in range(chunks):
        pltpu.make_async_copy(grad_ref.at[:, cols(side, c)], g_buf.at[0, c, mine, :], gx_sem.at[c]).start()
    for c in range(chunks):
        pltpu.make_async_copy(in_ref.at[:, cols(side, c)], u_buf.at[0, c, mine, :], ux_sem.at[c]).start()
    pltpu.make_async_copy(inv_hbm, inv, local_sem.at[2]).start()

    pl.semaphore_wait(barrier, 1 + jnp.minimum(level, 1))

    @pl.when(level > 0)
    def _():
        for c in range(chunks):
            remote(grad_ref.at[:, cols(side, c)], g_buf.at[1, c, mine, :], send_sem.at[1], direct_sem.at[c], left)

    for c in range(chunks):
        remote(grad_ref.at[:, cols(1 - side, c)], g_buf.at[0, c, mine, :], send_sem.at[0], gx_sem.at[c], mate)
    for c in range(chunks):
        remote(in_ref.at[:, cols(1 - side, c)], u_buf.at[0, c, mine, :], send_sem.at[0], ux_sem.at[c], mate)

    @at_level(1)
    def _():
        signal(ready, left)

    def forward(data):
        first = jnp.dot(fwd[0], data, preferred_element_type=jnp.float32)
        return first + jnp.dot(fwd[1], data, preferred_element_type=jnp.float32)

    def inverse():
        high, low = r_high[...], r_low[...]
        first = jnp.dot(inv[0], high, preferred_element_type=jnp.float32)
        second = jnp.dot(inv[1], high, preferred_element_type=jnp.float32)
        return first + (second + jnp.dot(inv[0], low, preferred_element_type=jnp.float32))

    def over_chunks(body):
        steps = block // 2 // CHUNK
        for sign, start in ((1.0, 0), (-1.0, steps)):
            def step(index, carry, sign=sign):
                row = pl.multiple_of(index * CHUNK, CHUNK)
                re, im = pl.ds(row, CHUNK), pl.ds(row + block, CHUNK)
                real, imag = body(re, im, sign)
                for place, value in ((re, real), (im, imag)):
                    top = value.astype(jnp.bfloat16)
                    r_high[place, :] = top
                    r_low[place, :] = (value - top.astype(jnp.float32)).astype(jnp.bfloat16)
                return carry
            lax.fori_loop(start, start + steps, step, 0)

    def against(a, b):
        return a[0] * b[0] + a[1] * b[1], a[1] * b[0] - a[0] * b[1]

    def plus(a, b):
        return a[0] + b[0], a[1] + b[1]

    def pair_sum(grads, values, c, pairs, re, im):
        total = None
        for i, j in pairs:
            term = against(
                (grads[i, c, re, :], grads[i, c, im, :]), (values[j, c, re, :], values[j, c, im, :])
            )
            total = term if total is None else plus(total, term)
        return total

    def lags_spectrum(c, near, far):
        def body(re, im, sign):
            total = pair_sum(g_spec, u_spec, c, near, re, im)
            if far:
                real, imag = pair_sum(g_spec, u_spec, c, far, re, im)
                total = total[0] - sign * imag, total[1] + sign * real
            return total
        over_chunks(body)
        return inverse()

    def in_grad(c, terms):
        def body(re, im, sign):
            taps = [(tap_spec[s, c, re, :], tap_spec[s, c, im, :]) for s in range(segs)]
            total = None
            for d in range(terms):
                real = imag = 0.0
                if d < segs:
                    real, imag = taps[d]
                if d > 0:
                    real = real + sign * taps[d - 1][1]
                    imag = imag - sign * taps[d - 1][0]
                term = against((g_spec[d, c, re, :], g_spec[d, c, im, :]), (real, imag))
                total = term if total is None else plus(total, term)
            return total
        over_chunks(body)
        in_buf[c] = inverse().astype(jnp.bfloat16)
        pltpu.make_async_copy(in_buf.at[c, mine, :], out_ref.at[:, cols(side, c)], out_sem.at[0]).start()
        remote(in_buf.at[c, other, :], out_ref.at[:, cols(side, c)], send_sem.at[0], out_sem.at[0], mate)

    def send_lags(c, at, owner_level, slot):
        for who in range(pair):
            owner = owner_level * pair + who
            piece = part.at[c, pl.ds(owner * own_lags, own_lags), :]
            target = lag_ref.at[slot, :, cols(side, c)]
            if owner_level != at:
                remote(piece, target, send_sem.at[2], lag_sem.at[slot], owner)
        if owner_level == at:
            def piece_of(owner):
                return part.at[c, rows(owner, own_lags), :]
            target = lag_ref.at[slot, :, cols(side, c)]
            remote(piece_of(mate), target, send_sem.at[2], lag_sem.at[slot], mate)
            pltpu.make_async_copy(piece_of(me), target, lag_sem.at[slot]).start()

    def tap_chunk(c):
        for s in range(segs):
            data = tap_buf[s * block:(s + 1) * block, c * width:(c + 1) * width]
            tap_spec[s, c] = forward(data)

    pltpu.make_async_copy(fwd_hbm, fwd, local_sem.at[0]).wait()
    wait_for(tap_buf, local_sem.at[1])
    tap_chunk(0)

    @at_level(0)
    def _():
        pl.semaphore_wait(ready, 1)
        for c in range(chunks):
            remote(in_ref.at[:, cols(side, c)], u_buf.at[1, c, mine, :], send_sem.at[1], left_u_sem.at[c], right)

    for c in range(1, chunks):
        tap_chunk(c)
    pltpu.make_async_copy(inv_hbm, inv, local_sem.at[2]).wait()

    def own_grads(c, at):
        wait_for(g_buf.at[0, c], gx_sem.at[c])
        if at > 0:
            remote(g_buf.at[0, c, other, :], g_buf.at[1, c, other, :], send_sem.at[1], passed_sem.at[c], left)
        g_spec[0, c] = forward(g_buf[0, c])

    def own_values(c, at):
        wait_for(u_buf.at[0, c], ux_sem.at[c])
        if at == 0:
            remote(u_buf.at[0, c, other, :], u_buf.at[1, c, other, :], send_sem.at[1], left_u_sem.at[c], right)
        u_spec[0, c] = forward(u_buf[0, c])

    def direct_grads(c, at):
        wait_for(g_buf.at[1, c, mine, :], direct_sem.at[c])
        if at > 0:
            remote(g_buf.at[1, c, mine, :], g_buf.at[2, c, mine, :], send_sem.at[1], far_sem.at[c], left)

    def passed_grads(c, at):
        wait_for(g_buf.at[1, c, other, :], passed_sem.at[c])
        if at > 0:
            remote(g_buf.at[1, c, other, :], g_buf.at[2, c, other, :], send_sem.at[1], far_sem.at[c], left)
        g_spec[1, c] = forward(g_buf[1, c])

    def far_grads(c):
        wait_for(g_buf.at[2, c], far_sem.at[c])
        g_spec[2, c] = forward(g_buf[2, c])

    def left_values(c):
        wait_for(u_buf.at[1, c], left_u_sem.at[c])
        u_spec[1, c] = forward(u_buf[1, c])

    every = range(chunks)
    low_rows, high_rows = pl.ds(0, block), pl.ds(block, block)

    @at_level(0)
    def _():
        for c in every:
            own_grads(c, 0)
        for c in every:
            own_values(c, 0)
            direct_grads(c, 0)
            passed_grads(c, 0)
            part[c, low_rows, :] = lags_spectrum(c, [(0, 0)], []).astype(jnp.bfloat16)
            send_lags(c, 0, 1, 0)
            send_lags(c, 0, 0, 0)
        for c in every:
            far_grads(c)
            in_grad(c, 3)

    @at_level(1)
    def _():
        for c in every:
            own_grads(c, 1)
        for c in every:
            direct_grads(c, 1)
            own_values(c, 1)
            passed_grads(c, 1)
        for c in every:
            left_values(c)
        signal(ready_far, right)
        for c in every:
            part[c, low_rows, :] = lags_spectrum(c, [(0, 0)], [(1, 0), (0, 1)]).astype(jnp.bfloat16)
            send_lags(c, 1, 0, 1)
            send_lags(c, 1, 1, 1)
        for c in every:
            far_grads(c)
            part[c, high_rows, :] = lags_spectrum(
                c, [(1, 0), (0, 1)], [(2, 0), (1, 1)]
            ).astype(jnp.bfloat16)
            send_lags(c, 1, 3, 0)
            send_lags(c, 1, 2, 0)
            in_grad(c, 3)

    @at_level(2)
    def _():
        lag_ref[2] = jnp.zeros(lag_ref.shape[1:], lag_ref.dtype)
        for c in every:
            own_grads(c, 2)
        for c in every:
            direct_grads(c, 2)
            own_values(c, 2)
            passed_grads(c, 2)
        for c in every:
            own_low[c] = lags_spectrum(c, [(0, 0)], [(1, 0)])
        pl.semaphore_wait(ready_far, 1)

        def finish_low(c):
            wait_for(next_low.at[c], low_sem.at[c])
            part[c, low_rows, :] = (own_low[c] + next_low[c].astype(jnp.float32)).astype(jnp.bfloat16)
            send_lags(c, 2, 0, 2)
            send_lags(c, 2, 1, 2)

        finish_low(0)
        for c in every:
            part[c, high_rows, :] = lags_spectrum(c, [(1, 0)], []).astype(jnp.bfloat16)
            send_lags(c, 2, 3, 1)
            send_lags(c, 2, 2, 1)
        for c in every[1:]:
            in_grad(c - 1, 2)
            finish_low(c)
        in_grad(chunks - 1, 2)

    @at_level(3)
    def _():
        lag_ref[2] = jnp.zeros(lag_ref.shape[1:], lag_ref.dtype)
        for c in every:
            own_grads(c, 3)
        for c in every:
            own_values(c, 3)
            part[c, low_rows, :] = lags_spectrum(c, [(0, 0)], []).astype(jnp.bfloat16)
            remote(part.at[c, low_rows, :], next_low.at[c], send_sem.at[1], low_sem.at[c], left)
        for c in every:
            in_grad(c, 1)

    wait_for(out_ref, out_sem.at[0])
    wait_for(lag_ref.at[0], lag_sem.at[0])
    wait_for(lag_ref.at[1], lag_sem.at[1])

    @at_level(0, 1)
    def _():
        wait_for(lag_ref.at[2], lag_sem.at[2])

    wait_for(g_buf.at[:, :, pl.ds(0, tok_len), :], send_sem.at[0])

    @at_level(0)
    def _():
        wait_for(g_buf.at[0], send_sem.at[1])
        wait_for(part.at[:, pl.ds(0, (levels // 2 * pair - 1) * own_lags), :], send_sem.at[2])

    @at_level(1, 2, 3)
    def _():
        wait_for(g_buf.at[pl.ds(0, 2)], send_sem.at[1])

    @at_level(1, 2)
    def _():
        wait_for(part.at[:, pl.ds(0, (levels * pair - 1) * own_lags), :], send_sem.at[2])


def rows_of_half(side, half):
    return pl.ds(pl.multiple_of(side * half, LANES), half)


def finish_kernel(in_ref, lag_ref, in_out, lag_out, lag_wide, sem):
    move = pltpu.make_async_copy(in_ref, in_out, sem.at[0])
    move.start()
    wide = [lag_ref[slot].astype(lag_wide.dtype) for slot in range(lag_ref.shape[0])]
    lag_wide[...] = wide[0] + wide[1] + wide[2]
    store = pltpu.make_async_copy(lag_wide, lag_out, sem.at[1])
    store.start()
    move.wait()
    store.wait()


PAIR = 2


def chain_fits(tok_len, channels, lag_count, count):
    block = PAIR * tok_len
    return (
        count % PAIR == 0
        and lag_count == 2 * block
        and count // PAIR == 2 * (lag_count // block)
        and channels % (PAIR * CHUNKS * LANES) == 0
        and tok_len % (2 * CHUNK) == 0
        and lag_count % (count * CHUNK) == 0
    )


def per_device(inputs, out_grad, filters):
    tok_len, channels = out_grad.shape
    lag_count = filters.shape[0]
    count = lax.axis_size("ctx")
    if not chain_fits(tok_len, channels, lag_count, count):
        return general_plan(inputs, out_grad, filters)
    block = PAIR * tok_len
    segs = lag_count // block
    half = channels // PAIR
    width = half // CHUNKS
    own_lags = lag_count // count
    fwd, inv = transform_tables(block)
    bf16, f32 = jnp.bfloat16, jnp.float32
    dma = pltpu.SemaphoreType.DMA
    anywhere = pl.BlockSpec(memory_space=pl.ANY)
    in_vmem = pl.BlockSpec(memory_space=pltpu.VMEM)
    in_grad, lag_grad = pl.pallas_call(
        functools.partial(chain_kernel, PAIR, block, CHUNKS),
        out_shape=(
            pltpu.VMEM((tok_len, channels), bf16),
            pltpu.VMEM((3, own_lags, channels), bf16),
        ),
        in_specs=[anywhere] * 5,
        out_specs=(in_vmem, in_vmem),
        scratch_shapes=[
            pltpu.VMEM((3, CHUNKS, block, width), bf16),
            pltpu.VMEM((2, CHUNKS, block, width), bf16),
            pltpu.VMEM((lag_count, half), bf16),
            pltpu.VMEM(fwd.shape, bf16),
            pltpu.VMEM(inv.shape, bf16),
            pltpu.VMEM((3, CHUNKS, 2 * block, width), f32),
            pltpu.VMEM((2, CHUNKS, 2 * block, width), f32),
            pltpu.VMEM((segs, CHUNKS, 2 * block, width), f32),
            pltpu.VMEM((2 * block, width), bf16),
            pltpu.VMEM((2 * block, width), bf16),
            pltpu.VMEM((CHUNKS, block, width), bf16),
            pltpu.VMEM((CHUNKS, lag_count, width), bf16),
            pltpu.VMEM((CHUNKS, block, width), f32),
            pltpu.VMEM((CHUNKS, block, width), bf16),
            dma((CHUNKS,)), dma((CHUNKS,)), dma((CHUNKS,)), dma((CHUNKS,)), dma((CHUNKS,)),
            dma((CHUNKS,)), dma((CHUNKS,)), dma((3,)), dma((1,)), dma((3,)), dma((3,)),
            pltpu.SemaphoreType.REGULAR,
            pltpu.SemaphoreType.REGULAR,
        ],
        compiler_params=pltpu.CompilerParams(collective_id=0, has_side_effects=True),
    )(inputs, out_grad, filters, jnp.asarray(fwd), jnp.asarray(inv))
    return pl.pallas_call(
        finish_kernel,
        out_shape=(
            jax.ShapeDtypeStruct(in_grad.shape, bf16),
            jax.ShapeDtypeStruct(lag_grad.shape[1:], f32),
        ),
        in_specs=[in_vmem, in_vmem],
        out_specs=(anywhere, anywhere),
        scratch_shapes=[
            pltpu.VMEM(lag_grad.shape[1:], f32),
            pltpu.SemaphoreType.DMA((2,)),
        ],
    )(
        pltpu.with_memory_space_constraint(in_grad, pltpu.VMEM),
        pltpu.with_memory_space_constraint(lag_grad, pltpu.VMEM),
    )


def solution(mesh):
    return jax.shard_map(
        per_device,
        mesh=mesh,
        in_specs=(P(("groups", "ctx"), "chan"), P(("groups", "ctx"), "chan"), P(None, "chan")),
        out_specs=(P(("groups", "ctx"), "chan"), P(("groups", "ctx"), "chan")),
        check_vma=False,
    )
```

time: 29 us -> 26.5 us (0.914)
  the two profiles are of different devices: /device:TPU:0 before, /device:TPU:12 now
where the time goes in v1:
time: 26.5 us; the launch traced here: 26.4 us
  Pallas kernels  25.7 us (97%)
  between operations  0.64 us (2%)
    pallas_call x1, Pallas kernels, per_device(): pl.pallas_call(functools.partial(chain_kernel, PAIR, block, CHUNKS), out_...  24.9 us
    pallas_call x1, Pallas kernels, per_device(): pl.pallas_call(finish_kernel, out_shape=(jax.ShapeDtypeStruct(in_grad.sha...  0.81 us

profile of v1, /device:TPU:12, one launch (start us, length us, event | category | flops | bytes accessed | tf_op | source)
XLA Modules:
  0.0 26.4 jit_solution(10213264745139628423)
XLA Ops:
  0.6 24.9 %shard_map.68 = (bf16[128,1024]{1,0:T(8,128)(2,1)S(1)}, bf16[3,64,1024]{2,1,0:T(8,128)(2,1)S(1)}) custom-call(bf16[128,1024]{1,0:T(8,128)(2,1)} %in_ref.1, bf16[128,1024]{1,0:T(8,128)(2,1)} %grad_ref.1, bf16[512,1024]{1,0:T(8,128)(2,1)} %taps_ref.1, bf16[2,512,256]{2,1,0:T(8,128)(2,1)} %constant.4.clone.fwd_hbm, bf16[2,256,512]{2,1,0:T(8,128)(2,1)} %constant.5.clone.inv_hbm), custom_call_target="tpu_custom_call" | custom-call | tf_op jit(solution)/shard_map/pallas_call | solution.py:495
  25.6 0.8 %shard_map.69 = (bf16[128,1024]{1,0:T(8,128)(2,1)}, f32[64,1024]{1,0:T(8,128)}) custom-call(bf16[128,1024]{1,0:T(8,128)(2,1)S(1)} %get-tuple-element.4.in_ref, bf16[3,64,1024]{2,1,0:T(8,128)(2,1)S(1)} %get-tuple-element.5.lag_ref), custom_call_target="tpu_custom_call" | custom-call | tf_op jit(solution)/shard_map/pallas_call | solution.py:525

commit v2 on v1

--- a/solution.py
+++ b/solution.py
@@ -12,6 +12,9 @@
 LANES = 128
 CHUNK = 16
 CHUNKS = 2
+FORWARD_PASSES = 1
+TAP_PASSES = 2
+INVERSE_PASSES = 1
 
 
 def passed_along(value, axis, steps):
@@ -134,9 +137,9 @@
     pair, block, chunks,
     in_ref, grad_ref, taps_ref, fwd_hbm, inv_hbm,
     out_ref, lag_ref,
-    g_buf, u_buf, tap_buf, fwd, inv, g_spec, u_spec, tap_spec, r_high, r_low, in_buf, part, own_low, next_low,
+    g_buf, u_buf, g_send, u_send, tap_buf, fwd, inv, g_spec, u_spec, tap_spec, r_high, r_low, in_buf, far_buf, in_sum, part, own_low, next_low,
     gx_sem, ux_sem, direct_sem, passed_sem, far_sem, left_u_sem, low_sem, lag_sem, out_sem, send_sem, local_sem,
-    ready, ready_far,
+    right_in, pair_in, far_in,
 ):
     me = lax.axis_index("ctx")
     level = lax.div(me, pair)
@@ -183,39 +186,47 @@
     def _():
         signal(barrier, right)
 
+    every = range(chunks)
+    whole = chunks // 2
+    for source, kept, sent, sem in (
+        (grad_ref, g_buf, g_send, local_sem.at[3]), (in_ref, u_buf, u_send, local_sem.at[4])
+    ):
+        for c in every:
+            pltpu.make_async_copy(source.at[:, cols(1 - side, c)], sent.at[c], sem).start()
+            pltpu.make_async_copy(source.at[:, cols(side, c)], kept.at[0, c, mine, :], sem).start()
+    pltpu.make_async_copy(fwd_hbm, fwd, local_sem.at[0]).start()
     pltpu.make_async_copy(taps_ref.at[:, rows_of_half(side, half)], tap_buf, local_sem.at[1]).start()
-    pltpu.make_async_copy(fwd_hbm, fwd, local_sem.at[0]).start()
-    for c in range(chunks):
-        pltpu.make_async_copy(grad_ref.at[:, cols(side, c)], g_buf.at[0, c, mine, :], gx_sem.at[c]).start()
-    for c in range(chunks):
-        pltpu.make_async_copy(in_ref.at[:, cols(side, c)], u_buf.at[0, c, mine, :], ux_sem.at[c]).start()
     pltpu.make_async_copy(inv_hbm, inv, local_sem.at[2]).start()
 
     pl.semaphore_wait(barrier, 1 + jnp.minimum(level, 1))
 
-    @pl.when(level > 0)
-    def _():
-        for c in range(chunks):
-            remote(grad_ref.at[:, cols(side, c)], g_buf.at[1, c, mine, :], send_sem.at[1], direct_sem.at[c], left)
-
-    for c in range(chunks):
-        remote(grad_ref.at[:, cols(1 - side, c)], g_buf.at[0, c, mine, :], send_sem.at[0], gx_sem.at[c], mate)
-    for c in range(chunks):
-        remote(in_ref.at[:, cols(1 - side, c)], u_buf.at[0, c, mine, :], send_sem.at[0], ux_sem.at[c], mate)
-
-    @at_level(1)
-    def _():
-        signal(ready, left)
-
-    def forward(data):
-        first = jnp.dot(fwd[0], data, preferred_element_type=jnp.float32)
-        return first + jnp.dot(fwd[1], data, preferred_element_type=jnp.float32)
+    def mate_grads(c):
+        remote(g_send.at[c], g_buf.at[0, c, mine, :], send_sem.at[0], gx_sem.at[c], mate)
+
+    def mate_values(c):
+        remote(u_send.at[c], u_buf.at[0, c, mine, :], send_sem.at[0], ux_sem.at[c], mate)
+
+    def grads_left(c):
+        remote(g_buf.at[0, c, mine, :], g_buf.at[1, c, mine, :], send_sem.at[1], direct_sem.at[c], left)
+
+    def values_right(c):
+        remote(u_buf.at[0, c, mine, :], u_buf.at[1, c, mine, :], send_sem.at[1], left_u_sem.at[c], right)
+
+    wait_for(g_buf.at[0], local_sem.at[3])
+
+    def forward(data, passes=FORWARD_PASSES):
+        total = jnp.dot(fwd[0], data, preferred_element_type=jnp.float32)
+        if passes > 1:
+            total = total + jnp.dot(fwd[1], data, preferred_element_type=jnp.float32)
+        return total
 
     def inverse():
-        high, low = r_high[...], r_low[...]
-        first = jnp.dot(inv[0], high, preferred_element_type=jnp.float32)
-        second = jnp.dot(inv[1], high, preferred_element_type=jnp.float32)
-        return first + (second + jnp.dot(inv[0], low, preferred_element_type=jnp.float32))
+        total = jnp.dot(inv[0], r_high[...], preferred_element_type=jnp.float32)
+        if INVERSE_PASSES > 1:
+            total = total + jnp.dot(inv[1], r_high[...], preferred_element_type=jnp.float32)
+        if INVERSE_PASSES > 2:
+            total = total + jnp.dot(inv[0], r_low[...], preferred_element_type=jnp.float32)
+        return total
 
     def over_chunks(body):
         steps = block // 2 // CHUNK
@@ -227,7 +238,8 @@
                 for place, value in ((re, real), (im, imag)):
                     top = value.astype(jnp.bfloat16)
                     r_high[place, :] = top
-                    r_low[place, :] = (value - top.astype(jnp.float32)).astype(jnp.bfloat16)
+                    if INVERSE_PASSES > 2:
+                        r_low[place, :] = (value - top.astype(jnp.float32)).astype(jnp.bfloat16)
                 return carry
             lax.fori_loop(start, start + steps, step, 0)
 
@@ -256,24 +268,31 @@
         over_chunks(body)
         return inverse()
 
-    def in_grad(c, terms):
+    def in_terms(c, terms):
         def body(re, im, sign):
             taps = [(tap_spec[s, c, re, :], tap_spec[s, c, im, :]) for s in range(segs)]
             total = None
-            for d in range(terms):
+            for i, d in terms:
                 real = imag = 0.0
                 if d < segs:
                     real, imag = taps[d]
                 if d > 0:
                     real = real + sign * taps[d - 1][1]
                     imag = imag - sign * taps[d - 1][0]
-                term = against((g_spec[d, c, re, :], g_spec[d, c, im, :]), (real, imag))
+                term = against((g_spec[i, c, re, :], g_spec[i, c, im, :]), (real, imag))
                 total = term if total is None else plus(total, term)
             return total
         over_chunks(body)
-        in_buf[c] = inverse().astype(jnp.bfloat16)
-        pltpu.make_async_copy(in_buf.at[c, mine, :], out_ref.at[:, cols(side, c)], out_sem.at[0]).start()
-        remote(in_buf.at[c, other, :], out_ref.at[:, cols(side, c)], send_sem.at[0], out_sem.at[0], mate)
+        return inverse().astype(jnp.bfloat16)
+
+    def out_place(c):
+        return out_ref.at[:, cols(side, c)]
+
+    def in_grad(c, terms, target):
+        in_buf[c] = in_terms(c, terms)
+        place = target
+        remote(in_buf.at[c, other, :], place, send_sem.at[0], out_sem.at[0], mate)
+        pltpu.make_async_copy(in_buf.at[c, mine, :], place, out_sem.at[0]).start()
 
     def send_lags(c, at, owner_level, slot):
         for who in range(pair):
@@ -292,137 +311,250 @@
     def tap_chunk(c):
         for s in range(segs):
             data = tap_buf[s * block:(s + 1) * block, c * width:(c + 1) * width]
-            tap_spec[s, c] = forward(data)
+            tap_spec[s, c] = forward(data, TAP_PASSES)
+
+    @at_level(1, 2)
+    def _():
+        signal(right_in, left)
+
+    @at_level(1, 2, 3)
+    def _():
+        for c in every:
+            mate_grads(c)
+
+            if c < whole:
+                grads_left(c)
+            else:
+                @at_level(2, 3)
+                def _():
+                    grads_left(c)
+
+    wait_for(u_buf.at[0], local_sem.at[4])
+    for c in every:
+        mate_values(c)
+
+    @at_level(0)
+    def _():
+        for c in every:
+            mate_grads(c)
 
     pltpu.make_async_copy(fwd_hbm, fwd, local_sem.at[0]).wait()
     wait_for(tap_buf, local_sem.at[1])
     tap_chunk(0)
 
-    @at_level(0)
-    def _():
-        pl.semaphore_wait(ready, 1)
-        for c in range(chunks):
-            remote(in_ref.at[:, cols(side, c)], u_buf.at[1, c, mine, :], send_sem.at[1], left_u_sem.at[c], right)
-
-    for c in range(1, chunks):
+    @at_level(0, 1)
+    def _():
+        pl.semaphore_wait(right_in, 1)
+        for c in every:
+            values_right(c)
+
+        @at_level(0)
+        def _():
+            signal(pair_in, right)
+
+    for c in every[1:]:
         tap_chunk(c)
+
+    @at_level(1)
+    def _():
+        pl.semaphore_wait(pair_in, 1)
+        signal(far_in, right)
+
     pltpu.make_async_copy(inv_hbm, inv, local_sem.at[2]).wait()
 
-    def own_grads(c, at):
-        wait_for(g_buf.at[0, c], gx_sem.at[c])
-        if at > 0:
+    def own_grads(c, pass_on):
+        wait_for(g_buf.at[0, c, other, :], gx_sem.at[c])
+        if pass_on:
             remote(g_buf.at[0, c, other, :], g_buf.at[1, c, other, :], send_sem.at[1], passed_sem.at[c], left)
-        g_spec[0, c] = forward(g_buf[0, c])
-
-    def own_values(c, at):
-        wait_for(u_buf.at[0, c], ux_sem.at[c])
-        if at == 0:
+
+    def own_values(c, pass_on):
+        wait_for(u_buf.at[0, c, other, :], ux_sem.at[c])
+        if pass_on:
             remote(u_buf.at[0, c, other, :], u_buf.at[1, c, other, :], send_sem.at[1], left_u_sem.at[c], right)
-        u_spec[0, c] = forward(u_buf[0, c])
-
-    def direct_grads(c, at):
+
+    def direct_grads(c, pass_on):
         wait_for(g_buf.at[1, c, mine, :], direct_sem.at[c])
-        if at > 0:
+        if pass_on:
             remote(g_buf.at[1, c, mine, :], g_buf.at[2, c, mine, :], send_sem.at[1], far_sem.at[c], left)
 
-    def passed_grads(c, at):
+    def passed_grads(c, pass_on):
         wait_for(g_buf.at[1, c, other, :], passed_sem.at[c])
-        if at > 0:
+        if pass_on:
             remote(g_buf.at[1, c, other, :], g_buf.at[2, c, other, :], send_sem.at[1], far_sem.at[c], left)
-        g_spec[1, c] = forward(g_buf[1, c])
+
+    def grads_spectrum(i, c):
+        g_spec[i, c] = forward(g_buf[i, c])
+
+    def values_spectrum(i, c):
+        u_spec[i, c] = forward(u_buf[i, c])
 
     def far_grads(c):
         wait_for(g_buf.at[2, c], far_sem.at[c])
-        g_spec[2, c] = forward(g_buf[2, c])
+        grads_spectrum(2, c)
 
     def left_values(c):
         wait_for(u_buf.at[1, c], left_u_sem.at[c])
-        u_spec[1, c] = forward(u_buf[1, c])
-
-    every = range(chunks)
+        values_spectrum(1, c)
+
     low_rows, high_rows = pl.ds(0, block), pl.ds(block, block)
+    low_owners = levels // 2 * pair
+    turns = [
+        (c, owner) for first in range(0, low_owners, pair) for c in every for owner in range(first, first + pair)
+    ]
 
     @at_level(0)
     def _():
         for c in every:
-            own_grads(c, 0)
-        for c in every:
-            own_values(c, 0)
-            direct_grads(c, 0)
-            passed_grads(c, 0)
+            own_values(c, True)
+            values_spectrum(0, c)
+        for c in every:
+            own_grads(c, False)
+            grads_spectrum(0, c)
             part[c, low_rows, :] = lags_spectrum(c, [(0, 0)], []).astype(jnp.bfloat16)
+            send_lags(c, 0, 0, 0)
+        for c in every[whole:]:
+            in_grad(c, [(0, 0)], in_sum.at[0, side, c - whole])
+        for c in every[:whole]:
+            direct_grads(c, False)
+            passed_grads(c, False)
+            grads_spectrum(1, c)
+        for c in every:
             send_lags(c, 0, 1, 0)
-            send_lags(c, 0, 0, 0)
-        for c in every:
+        for c in every[:whole]:
             far_grads(c)
-            in_grad(c, 3)
+            in_grad(c, [(0, 0), (1, 1), (2, 2)], out_place(c))
 
     @at_level(1)
     def _():
         for c in every:
-            own_grads(c, 1)
-        for c in every:
-            direct_grads(c, 1)
-            own_values(c, 1)
-            passed_grads(c, 1)
-        for c in every:
+            own_grads(c, c < whole)
+            grads_spectrum(0, c)
+        for c in every:
+            direct_grads(c, c < whole)
+        for c in every:
+            own_values(c, True)
+            values_spectrum(0, c)
+
+        def low(c):
             left_values(c)
-        signal(ready_far, right)
-        for c in every:
-            part[c, low_rows, :] = lags_spectrum(c, [(0, 0)], [(1, 0), (0, 1)]).astype(jnp.bfloat16)
-            send_lags(c, 1, 0, 1)
+            part[c, low_rows, :] = lags_spectrum(c, [(0, 0)], [(0, 1)]).astype(jnp.bfloat16)
+            low_to(c, 0)
+
+        def low_to(c, owner):
+            piece = part.at[c, pl.ds(owner * own_lags, own_lags), :]
+            remote(piece, lag_ref.at[1, :, cols(side, c)], send_sem.at[2], lag_sem.at[1], owner)
+
+        def far_to(c, owner):
+            remote(
+                far_buf.at[c - whole, pl.ds(owner * tok_len, tok_len), :], in_sum.at[1, side, c - whole],
+                send_sem.at[3], out_sem.at[1], owner,
+            )
+
+        def passed(c):
+            passed_grads(c, c < whole)
+            grads_spectrum(1, c)
+            if c >= whole:
+                far_buf[c - whole] = in_terms(c, [(0, 1), (1, 2)])
+                far_to(c, 0)
+
+        low(0)
+        for c in every[1:]:
+            passed(c - 1)
+            low(c)
+        passed(chunks - 1)
+        for owner in range(1, pair):
+            for c in every[whole:]:
+                far_to(c, owner)
+            for c in every:
+                low_to(c, owner)
+        for c in every:
             send_lags(c, 1, 1, 1)
         for c in every:
+            part[c, high_rows, :] = lags_spectrum(c, [(0, 1)], [(1, 1)]).astype(jnp.bfloat16)
+        for c in every:
             far_grads(c)
-            part[c, high_rows, :] = lags_spectrum(
-                c, [(1, 0), (0, 1)], [(2, 0), (1, 1)]
-            ).astype(jnp.bfloat16)
             send_lags(c, 1, 3, 0)
             send_lags(c, 1, 2, 0)
-            in_grad(c, 3)
+            in_grad(c, [(0, 0), (1, 1), (2, 2)], out_place(c))
 
     @at_level(2)
     def _():
         lag_ref[2] = jnp.zeros(lag_ref.shape[1:], lag_ref.dtype)
         for c in every:
-            own_grads(c, 2)
-        for c in every:
-            direct_grads(c, 2)
-            own_values(c, 2)
-            passed_grads(c, 2)
-        for c in every:
-            own_low[c] = lags_spectrum(c, [(0, 0)], [(1, 0)])
-        pl.semaphore_wait(ready_far, 1)
-
-        def finish_low(c):
-            wait_for(next_low.at[c], low_sem.at[c])
-            part[c, low_rows, :] = (own_low[c] + next_low[c].astype(jnp.float32)).astype(jnp.bfloat16)
-            send_lags(c, 2, 0, 2)
-            send_lags(c, 2, 1, 2)
-
-        finish_low(0)
-        for c in every:
-            part[c, high_rows, :] = lags_spectrum(c, [(1, 0)], []).astype(jnp.bfloat16)
+            own_grads(c, True)
+            grads_spectrum(0, c)
+        direct_grads(0, True)
+        for c in every:
+            own_values(c, False)
+            values_spectrum(0, c)
+        for c in every:
+            passed_grads(c, True)
+            if c + 1 < chunks:
+                direct_grads(c + 1, True)
+            grads_spectrum(1, c)
+            if c == 0:
+                in_grad(0, [(0, 0), (1, 1)], out_place(0))
+        for c in every:
+            left_values(c)
+            own_low[c] = lags_spectrum(c, [(0, 0)], [(1, 0), (0, 1)])
+        pl.semaphore_wait(far_in, 1)
+
+        def finish_low(c, owner):
+            piece = pl.ds(owner * own_lags, own_lags)
+            wait_for(next_low.at[c, piece, :], low_sem.at[c, owner])
+            total = own_low[c, piece, :] + next_low[c, piece, :].astype(jnp.float32)
+            part[c, piece, :] = total.astype(jnp.bfloat16)
+            remote(part.at[c, piece, :], lag_ref.at[2, :, cols(side, c)], send_sem.at[2], lag_sem.at[2], owner)
+
+        def high(c):
+            part[c, high_rows, :] = lags_spectrum(c, [(1, 0), (0, 1)], [(1, 1)]).astype(jnp.bfloat16)
             send_lags(c, 2, 3, 1)
             send_lags(c, 2, 2, 1)
+
+        half_way = len(turns) // 2
+        for turn in sorted(turns[:half_way], key=lambda turn: turn[1]):
+            finish_low(*turn)
+        high(0)
+        for turn in turns[half_way:]:
+            finish_low(*turn)
         for c in every[1:]:
-            in_grad(c - 1, 2)
-            finish_low(c)
-        in_grad(chunks - 1, 2)
+            high(c)
+        for c in every[1:]:
+            in_grad(c, [(0, 0), (1, 1)], out_place(c))
 
     @at_level(3)
     def _():
         lag_ref[2] = jnp.zeros(lag_ref.shape[1:], lag_ref.dtype)
-        for c in every:
-            own_grads(c, 3)
-        for c in every:
-            own_values(c, 3)
+
+        def next_level_low(c, owner):
+            piece = pl.ds(owner * own_lags, own_lags)
+            remote(part.at[c, piece, :], next_low.at[c, piece, :], send_sem.at[1], low_sem.at[c, owner], left)
+
+        for c in every:
+            own_grads(c, True)
+            grads_spectrum(0, c)
+        for c in every:
+            own_values(c, False)
+            values_spectrum(0, c)
             part[c, low_rows, :] = lags_spectrum(c, [(0, 0)], []).astype(jnp.bfloat16)
-            remote(part.at[c, low_rows, :], next_low.at[c], send_sem.at[1], low_sem.at[c], left)
-        for c in every:
-            in_grad(c, 1)
+            for owner in range(pair):
+                next_level_low(c, owner)
+        for c, owner in turns[pair * chunks:]:
+            next_level_low(c, owner)
+        for c in every:
+            in_grad(c, [(0, 0)], out_place(c))
 
     wait_for(out_ref, out_sem.at[0])
+
+    @at_level(0)
+    def _():
+        wait_for(in_sum.at[1], out_sem.at[1])
+        for which in range(pair):
+            for c in every[whole:]:
+                at = which * half + c * width
+                total = in_sum[0, which, c - whole].astype(jnp.float32) + in_sum[1, which, c - whole].astype(jnp.float32)
+                out_ref[:, at:at + width] = total.astype(out_ref.dtype)
+
     wait_for(lag_ref.at[0], lag_sem.at[0])
     wait_for(lag_ref.at[1], lag_sem.at[1])
 
@@ -440,6 +572,10 @@
     @at_level(1, 2, 3)
     def _():
         wait_for(g_buf.at[pl.ds(0, 2)], send_sem.at[1])
+
+    @at_level(1)
+    def _():
+        wait_for(far_buf, send_sem.at[3])
 
     @at_level(1, 2)
     def _():
@@ -503,6 +639,8 @@
         scratch_shapes=[
             pltpu.VMEM((3, CHUNKS, block, width), bf16),
             pltpu.VMEM((2, CHUNKS, block, width), bf16),
+            pltpu.VMEM((CHUNKS, tok_len, width), bf16),
+            pltpu.VMEM((CHUNKS, tok_len, width), bf16),
             pltpu.VMEM((lag_count, half), bf16),
             pltpu.VMEM(fwd.shape, bf16),
             pltpu.VMEM(inv.shape, bf16),
@@ -512,11 +650,14 @@
             pltpu.VMEM((2 * block, width), bf16),
             pltpu.VMEM((2 * block, width), bf16),
             pltpu.VMEM((CHUNKS, block, width), bf16),
+            pltpu.VMEM((CHUNKS // 2, block, width), bf16),
+            pltpu.VMEM((2, PAIR, CHUNKS // 2, tok_len, width), bf16),
             pltpu.VMEM((CHUNKS, lag_count, width), bf16),
             pltpu.VMEM((CHUNKS, block, width), f32),
             pltpu.VMEM((CHUNKS, block, width), bf16),
             dma((CHUNKS,)), dma((CHUNKS,)), dma((CHUNKS,)), dma((CHUNKS,)), dma((CHUNKS,)),
-            dma((CHUNKS,)), dma((CHUNKS,)), dma((3,)), dma((1,)), dma((3,)), dma((3,)),
+            dma((CHUNKS,)), dma((CHUNKS, count // 2)), dma((3,)), dma((2,)), dma((4,)), dma((5,)),
+            pltpu.SemaphoreType.REGULAR,
             pltpu.SemaphoreType.REGULAR,
             pltpu.SemaphoreType.REGULAR,
         ],

time: 26.5 us -> 23.5 us (0.89)
  Pallas kernels: 25.7 us -> 22.7 us
    pallas_call x1, Pallas kernels: 24.9 us -> 21.9 us  [per_device(): pl.pallas_call(functools.partial(chain_kernel, PAIR, block, CHUNKS), out_...]
where the time goes in v2:
time: 23.5 us; the launch traced here: 23.3 us
  Pallas kernels  22.7 us (97%)
  between operations  0.64 us (3%)
    pallas_call x1, Pallas kernels, per_device(): pl.pallas_call(functools.partial(chain_kernel, PAIR, block, CHUNKS), out_...  21.9 us
    pallas_call x1, Pallas kernels, per_device(): pl.pallas_call(finish_kernel, out_shape=(jax.ShapeDtypeStruct(in_grad.sha...  0.81 us

profile of v2, /device:TPU:12, one launch (start us, length us, event | category | flops | bytes accessed | tf_op | source)
XLA Modules:
  0.0 23.3 jit_solution(11601122975443751826)
XLA Ops:
  0.6 21.9 %shard_map.68 = (bf16[128,1024]{1,0:T(8,128)(2,1)S(1)}, bf16[3,64,1024]{2,1,0:T(8,128)(2,1)S(1)}) custom-call(bf16[128,1024]{1,0:T(8,128)(2,1)} %in_ref.1, bf16[128,1024]{1,0:T(8,128)(2,1)} %grad_ref.1, bf16[512,1024]{1,0:T(8,128)(2,1)} %taps_ref.1, bf16[2,512,256]{2,1,0:T(8,128)(2,1)} %constant.4.clone.fwd_hbm, bf16[2,256,512]{2,1,0:T(8,128)(2,1)} %constant.5.clone.inv_hbm), custom_call_target="tpu_custom_call" | custom-call | tf_op jit(solution)/shard_map/pallas_call | solution.py:631
  22.5 0.8 %shard_map.69 = (bf16[128,1024]{1,0:T(8,128)(2,1)}, f32[64,1024]{1,0:T(8,128)}) custom-call(bf16[128,1024]{1,0:T(8,128)(2,1)S(1)} %get-tuple-element.4.in_ref, bf16[3,64,1024]{2,1,0:T(8,128)(2,1)S(1)} %get-tuple-element.5.lag_ref), custom_call_target="tpu_custom_call" | custom-call | tf_op jit(solution)/shard_map/pallas_call | solution.py:666

commit v3 on v2

--- a/solution.py
+++ b/solution.py
@@ -137,7 +137,7 @@
     pair, block, chunks,
     in_ref, grad_ref, taps_ref, fwd_hbm, inv_hbm,
     out_ref, lag_ref,
-    g_buf, u_buf, g_send, u_send, tap_buf, fwd, inv, g_spec, u_spec, tap_spec, r_high, r_low, in_buf, far_buf, in_sum, part, own_low, next_low,
+    g_buf, u_buf, g_send, u_send, tap_buf, fwd, inv, g_spec, u_spec, tap_spec, sum_spec, r_high, r_low, in_buf, far_buf, in_sum, part, own_low, next_low,
     gx_sem, ux_sem, direct_sem, passed_sem, far_sem, left_u_sem, low_sem, lag_sem, out_sem, send_sem, local_sem,
     right_in, pair_in, far_in,
 ):
@@ -220,22 +220,23 @@
             total = total + jnp.dot(fwd[1], data, preferred_element_type=jnp.float32)
         return total
 
-    def inverse():
-        total = jnp.dot(inv[0], r_high[...], preferred_element_type=jnp.float32)
+    def inverse(which=None):
+        places = slice(None) if which is None else which
+        total = jnp.dot(inv[0, places, :], r_high[...], preferred_element_type=jnp.float32)
         if INVERSE_PASSES > 1:
-            total = total + jnp.dot(inv[1], r_high[...], preferred_element_type=jnp.float32)
+            total = total + jnp.dot(inv[1, places, :], r_high[...], preferred_element_type=jnp.float32)
         if INVERSE_PASSES > 2:
-            total = total + jnp.dot(inv[0], r_low[...], preferred_element_type=jnp.float32)
+            total = total + jnp.dot(inv[0, places, :], r_low[...], preferred_element_type=jnp.float32)
         return total
 
-    def over_chunks(body):
+    def over_chunks(body, split=True):
         steps = block // 2 // CHUNK
         for sign, start in ((1.0, 0), (-1.0, steps)):
             def step(index, carry, sign=sign):
                 row = pl.multiple_of(index * CHUNK, CHUNK)
                 re, im = pl.ds(row, CHUNK), pl.ds(row + block, CHUNK)
-                real, imag = body(re, im, sign)
-                for place, value in ((re, real), (im, imag)):
+                spectrum = body(re, im, sign)
+                for place, value in zip((re, im), spectrum if split else ()):
                     top = value.astype(jnp.bfloat16)
                     r_high[place, :] = top
                     if INVERSE_PASSES > 2:
@@ -268,31 +269,42 @@
         over_chunks(body)
         return inverse()
 
-    def in_terms(c, terms):
+    def in_spectrum(c, terms, sign, re, im):
+        taps = [(tap_spec[s, c, re, :], tap_spec[s, c, im, :]) for s in range(segs)]
+        total = None
+        for i, d in terms:
+            real = imag = 0.0
+            if d < segs:
+                real, imag = taps[d]
+            if d > 0:
+                real = real + sign * taps[d - 1][1]
+                imag = imag - sign * taps[d - 1][0]
+            term = against((g_spec[i, c, re, :], g_spec[i, c, im, :]), (real, imag))
+            total = term if total is None else plus(total, term)
+        return total
+
+    def in_terms(c, terms, summed=False):
         def body(re, im, sign):
-            taps = [(tap_spec[s, c, re, :], tap_spec[s, c, im, :]) for s in range(segs)]
-            total = None
-            for i, d in terms:
-                real = imag = 0.0
-                if d < segs:
-                    real, imag = taps[d]
-                if d > 0:
-                    real = real + sign * taps[d - 1][1]
-                    imag = imag - sign * taps[d - 1][0]
-                term = against((g_spec[i, c, re, :], g_spec[i, c, im, :]), (real, imag))
-                total = term if total is None else plus(total, term)
+            total = in_spectrum(c, terms, sign, re, im)
+            if summed:
+                total = plus(total, (sum_spec[c, re, :], sum_spec[c, im, :]))
             return total
         over_chunks(body)
-        return inverse().astype(jnp.bfloat16)
+
+    def sum_ready(c):
+        def body(re, im, sign):
+            sum_spec[c, re, :], sum_spec[c, im, :] = in_spectrum(c, [(0, 0), (1, 1)], sign, re, im)
+        over_chunks(body, False)
 
     def out_place(c):
         return out_ref.at[:, cols(side, c)]
 
-    def in_grad(c, terms, target):
-        in_buf[c] = in_terms(c, terms)
-        place = target
-        remote(in_buf.at[c, other, :], place, send_sem.at[0], out_sem.at[0], mate)
-        pltpu.make_async_copy(in_buf.at[c, mine, :], place, out_sem.at[0]).start()
+    def in_grad(c, terms, target, summed=False):
+        in_terms(c, terms, summed)
+        in_buf[0, c] = inverse(other).astype(jnp.bfloat16)
+        remote(in_buf.at[0, c], target, send_sem.at[0], out_sem.at[0], mate)
+        in_buf[1, c] = inverse(mine).astype(jnp.bfloat16)
+        pltpu.make_async_copy(in_buf.at[1, c], target, out_sem.at[0]).start()
 
     def send_lags(c, at, owner_level, slot):
         for who in range(pair):
@@ -421,8 +433,9 @@
         for c in every:
             send_lags(c, 0, 1, 0)
         for c in every[:whole]:
+            sum_ready(c)
             far_grads(c)
-            in_grad(c, [(0, 0), (1, 1), (2, 2)], out_place(c))
+            in_grad(c, [(2, 2)], out_place(c), True)
 
     @at_level(1)
     def _():
@@ -454,7 +467,8 @@
             passed_grads(c, c < whole)
             grads_spectrum(1, c)
             if c >= whole:
-                far_buf[c - whole] = in_terms(c, [(0, 1), (1, 2)])
+                in_terms(c, [(0, 1), (1, 2)])
+                far_buf[c - whole] = inverse().astype(jnp.bfloat16)
                 far_to(c, 0)
 
         low(0)
@@ -472,10 +486,14 @@
         for c in every:
             part[c, high_rows, :] = lags_spectrum(c, [(0, 1)], [(1, 1)]).astype(jnp.bfloat16)
         for c in every:
+            sum_ready(c)
+        for c in every:
             far_grads(c)
-            send_lags(c, 1, 3, 0)
-            send_lags(c, 1, 2, 0)
-            in_grad(c, [(0, 0), (1, 1), (2, 2)], out_place(c))
+            if c == 0:
+                for b in every:
+                    send_lags(b, 1, 3, 0)
+                    send_lags(b, 1, 2, 0)
+            in_grad(c, [(2, 2)], out_place(c), True)
 
     @at_level(2)
     def _():
@@ -483,18 +501,13 @@
         for c in every:
             own_grads(c, True)
             grads_spectrum(0, c)
-        direct_grads(0, True)
+            direct_grads(c, True)
         for c in every:
             own_values(c, False)
             values_spectrum(0, c)
         for c in every:
             passed_grads(c, True)
-            if c + 1 < chunks:
-                direct_grads(c + 1, True)
             grads_spectrum(1, c)
-            if c == 0:
-                in_grad(0, [(0, 0), (1, 1)], out_place(0))
-        for c in every:
             left_values(c)
             own_low[c] = lags_spectrum(c, [(0, 0)], [(1, 0), (0, 1)])
         pl.semaphore_wait(far_in, 1)
@@ -512,14 +525,16 @@
             send_lags(c, 2, 2, 1)
 
         half_way = len(turns) // 2
-        for turn in sorted(turns[:half_way], key=lambda turn: turn[1]):
+        first = sorted(turns[:half_way], key=lambda turn: turn[1])
+        finish_low(*first[0])
+        in_grad(0, [(0, 0), (1, 1)], out_place(0))
+        for turn in first[1:]:
             finish_low(*turn)
         high(0)
         for turn in turns[half_way:]:
             finish_low(*turn)
         for c in every[1:]:
             high(c)
-        for c in every[1:]:
             in_grad(c, [(0, 0), (1, 1)], out_place(c))
 
     @at_level(3)
@@ -647,9 +662,10 @@
             pltpu.VMEM((3, CHUNKS, 2 * block, width), f32),
             pltpu.VMEM((2, CHUNKS, 2 * block, width), f32),
             pltpu.VMEM((segs, CHUNKS, 2 * block, width), f32),
+            pltpu.VMEM((CHUNKS, 2 * block, width), f32),
             pltpu.VMEM((2 * block, width), bf16),
             pltpu.VMEM((2 * block, width), bf16),
-            pltpu.VMEM((CHUNKS, block, width), bf16),
+            pltpu.VMEM((2, CHUNKS, tok_len, width), bf16),
             pltpu.VMEM((CHUNKS // 2, block, width), bf16),
             pltpu.VMEM((2, PAIR, CHUNKS // 2, tok_len, width), bf16),
             pltpu.VMEM((CHUNKS, lag_count, width), bf16),

time: 23.5 us -> 23.4 us (level); the launches traced: 23.3 us -> 22.9 us
  Pallas kernels: 22.7 us -> 22.3 us
    pallas_call x1, Pallas kernels: 21.9 us -> 21.5 us  [per_device(): pl.pallas_call(functools.partial(chain_kernel, PAIR, block, CHUNKS), out_...]
where the time goes in v3:
time: 23.4 us; the launch traced here: 22.9 us
  Pallas kernels  22.3 us (95%)
  between operations  0.64 us (3%)
    pallas_call x1, Pallas kernels, per_device(): pl.pallas_call(functools.partial(chain_kernel, PAIR, block, CHUNKS), out_...  21.5 us
    pallas_call x1, Pallas kernels, per_device(): pl.pallas_call(finish_kernel, out_shape=(jax.ShapeDtypeStruct(in_grad.sha...  0.81 us

profile of v3, /device:TPU:12, one launch (start us, length us, event | category | flops | bytes accessed | tf_op | source)
XLA Modules:
  0.0 22.9 jit_solution(445674722375736873)
XLA Ops:
  0.6 21.5 %shard_map.68 = (bf16[128,1024]{1,0:T(8,128)(2,1)S(1)}, bf16[3,64,1024]{2,1,0:T(8,128)(2,1)S(1)}) custom-call(bf16[128,1024]{1,0:T(8,128)(2,1)} %in_ref.1, bf16[128,1024]{1,0:T(8,128)(2,1)} %grad_ref.1, bf16[512,1024]{1,0:T(8,128)(2,1)} %taps_ref.1, bf16[2,512,256]{2,1,0:T(8,128)(2,1)} %constant.4.clone.fwd_hbm, bf16[2,256,512]{2,1,0:T(8,128)(2,1)} %constant.5.clone.inv_hbm), custom_call_target="tpu_custom_call" | custom-call | tf_op jit(solution)/shard_map/pallas_call | solution.py:646
  22.1 0.8 %shard_map.69 = (bf16[128,1024]{1,0:T(8,128)(2,1)}, f32[64,1024]{1,0:T(8,128)}) custom-call(bf16[128,1024]{1,0:T(8,128)(2,1)S(1)} %get-tuple-element.4.in_ref, bf16[3,64,1024]{2,1,0:T(8,128)(2,1)S(1)} %get-tuple-element.5.lag_ref), custom_call_target="tpu_custom_call" | custom-call | tf_op jit(solution)/shard_map/pallas_call | solution.py:682
